TPU v7x, 32 devices: a whole 2x2x4 slice. The times are simulated.
32 devices in a mesh: groups: 2 (over y), frame: 4 (over z), panel: 2 (over x), sub: 2 (over core).
Axes of the slice: x: 2, y: 2, z: 4, core: 2. Of those that a mesh axis runs over, the one named last changes fastest.
Arguments:
- frames: bfloat16 [2048, 65536], P(('groups', 'frame'), ('panel', 'sub')), parts along dimension 0, may hold values from -16 to 16
- slices: float32 [32, 65536], P(('groups', 'frame'), ('panel', 'sub')), parts along dimension 0, may hold values from -8 to 8
- log_prior: float32 [4096], replicated, may hold values from -2 to 2
- orient: int32 [32], P('groups'), parts along dimension 0, may hold values from 0 to 4095
Outputs:
- new_slices: float32 [32, 65536], P(('groups', 'frame'), ('panel', 'sub')), parts along dimension 0
There are 2 independent parts, one for each index of `groups`. A program takes and returns all parts, laid end to end along the dimension named above; an argument that names none is the same for every part. Nothing has to cross between parts.
All inputs are finite; a program needn't handle non-finite values.
Results may differ from a plain program's by a relative error of at most 0.022.
The roundings to bfloat16 on the way count: a program that leaves them out, or rounds other values in their place, can miss the bound.
Values may be sent and summed in bfloat16 or wider, within the bound.
A program may use at most 64 MiB of HBM per device.

v0:
```python
import math
import jax
import jax.numpy as jnp
from jax import lax
from jax.sharding import PartitionSpec as P

PIX = 65536
ITERS = 2


def fetch_slices(owned_b):
    return lax.all_gather(owned_b, "frame", axis=0, tiled=True)


def owner_update(weights, frames, counts, owned_b, offset):
    owned = owned_b.shape[0]
    mine = lax.psum_scatter(
        jnp.einsum("fm,fp->mp", weights, frames, preferred_element_type=jnp.float32).astype(
            jnp.bfloat16
        ),
        "frame",
        scatter_dimension=0,
        tiled=True,
    ).astype(jnp.float32)
    my_counts = lax.dynamic_slice_in_dim(counts, offset, owned, 0)
    return (mine + owned_b.astype(jnp.float32)) / (my_counts + 1.0)[:, None]


def local(frames, slices, log_prior, orient):
    owned = slices.shape[0]
    temper = 3.0 / math.sqrt(PIX)
    matches = orient[:, None] == jnp.arange(log_prior.shape[0], dtype=jnp.int32)[None, :]
    prior = jnp.sum(jnp.where(matches, log_prior[None, :], 0.0), axis=1)
    offset = lax.axis_index("frame") * owned
    current = slices
    owned_b = slices.astype(jnp.bfloat16)
    for step in range(ITERS):
        if step == 0:
            gathered = fetch_slices(owned_b)
        else:
            gathered = fetch_slices(owned_b)
        wide = gathered.astype(jnp.float32)
        norms = jnp.sum(wide * wide, axis=1)
        raw = (
            jnp.einsum("fp,mp->fm", frames, gathered, preferred_element_type=jnp.float32)
            - 0.5 * norms[None, :]
        )
        summed = lax.psum(raw, ("panel", "sub"))
        weights = jax.nn.softmax(temper * summed + prior[None, :], axis=1).astype(jnp.bfloat16)
        counts = lax.psum(jnp.sum(weights.astype(jnp.float32), axis=0), "frame")
        if step + 1 < ITERS:
            current = owner_update(weights, frames, counts, owned_b, offset)
            owned_b = current.astype(jnp.bfloat16)
        else:
            current = owner_update(weights, frames, counts, owned_b, offset)
    return current


def solution(mesh):
    in_specs = (
        P(("groups", "frame"), ("panel", "sub")),
        P(("groups", "frame"), ("panel", "sub")),
        P(),
        P("groups"),
    )
    out_specs = P(("groups", "frame"), ("panel", "sub"))
    return jax.shard_map(local, mesh=mesh, in_specs=in_specs, out_specs=out_specs, check_vma=False)
```

profile of v0, /device:TPU:0, one launch (start us, length us, event | category | flops | bytes accessed | tf_op | source)
XLA Modules:
  0.0 173.9 jit_solution(4613914813418080331)
XLA Ops:
  6.5 0.0 copy-start.2
  6.5 0.0 copy-start.1
  6.5 0.0 all-reduce.5.cloned.1.call-start
  6.5 1.0 convert_bitcast_fusion
  7.6 17.4 %all-gather = bf16[4,4,16384]{2,1,0:T(4,128)(2,1)S(1)} all-gather(bf16[1,4,16384]{2,1,0:T(4,128)(2,1)S(1)} %convert_bitcast_fusion), channel_id=1, replica_groups=mesh['groups'=2,'frame'=4,'panel'=2,'sub'=2] {'frame'}, dimensions={0}, use_global_device_ids=true | all-gather | bytes 655360 | tf_op jit(solution)/shard_map/all_gather | solution.py:12
  24.9 0.1 reshape.18
  25.1 0.2 multiply_reduce_fusion.1
  25.3 0.0 copy-start.3
  25.3 0.0 copy-start
  25.3 5.7 %convolution_subtract_fusion.1 = f32[256,16]{0,1:T(8,128)S(1)} fusion(bf16[256,16384]{1,0:T(8,128)(2,1)} %param.4, bf16[16,16384]{1,0:T(8,128)(2,1)S(1)} %reshape.18, f32[16]{0:T(128)S(1)} %broadcast_multiply_fusion.1), kind=kOutput, calls=%fused_computation.4 | convolution fusion | flops 134221824 | bytes 8929344 | tf_op jit(solution)/shard_map/fp,mp->fm/dot_general | solution.py:45
  31.0 10.1 %psum.28 = f32[256,16]{0,1:T(8,128)S(1)} all-reduce(f32[256,16]{0,1:T(8,128)S(1)} %convolution_subtract_fusion.1), channel_id=1, replica_groups=mesh['groups'=2,'frame'=4,'panel'=2,'sub'=2] {'panel','sub'}, use_global_device_ids=true, to_apply=%region_1.2 | all-reduce | flops 4096 | bytes 32768 | tf_op jit(solution)/shard_map/psum | solution.py:48
  41.1 0.0 copy-done.2
  41.1 0.0 copy-done.1
  41.1 0.2 select_reduce_fusion
  41.4 0.1 fusion.2
  41.5 0.1 fusion.4
  41.6 0.2 convert_reduce_fusion.1
  41.7 5.4 %convolution_convert_fusion.1 = bf16[16,16384]{1,0:T(8,128)(2,1)} fusion(bf16[256,16]{0,1:T(8,128)(2,1)S(1)} %get-tuple-element.8, bf16[256,16384]{1,0:T(8,128)(2,1)} %param.4), kind=kOutput, calls=%fused_computation.1 | convolution fusion | flops 134479872 | bytes 8921088 | tf_op jit(solution)/shard_map/fm,fp->mp/dot_general | solution.py:18
  47.2 0.0 all-reduce.5.cloned.1.call-update
  47.2 0.0 all-reduce.7.cloned.1.call-start
  47.2 0.0 copy-done.3
  47.3 0.6 dynamic-slice
  48.5 12.6 %psum.29 = f32[16]{0:T(128)S(1)} all-reduce(f32[16]{0:T(128)S(1)} %get-tuple-element.7), channel_id=1, replica_groups=mesh['groups'=2,'frame'=4,'panel'=2,'sub'=2] {'frame'}, use_global_device_ids=true, to_apply=%region_7.8 | all-reduce | flops 16 | bytes 128 | tf_op jit(solution)/shard_map/psum | solution.py:50
  61.0 0.1 dynamic-slice_add_fusion.1
  61.1 26.4 %all-reduce.5.cloned.1.call-done = bf16[16,16384]{1,0:T(8,128)(2,1)} async-done(((bf16[16,16384]{1,0:T(8,128)(2,1)}), bf16[16,16384]{1,0:T(8,128)(2,1)}) %all-reduce.5.cloned.1.call-update) | async-done | bytes 524304
  87.6 0.0 copy-done
  87.6 1.1 fusion.1
  88.6 16.2 %all-gather.1 = bf16[4,4,16384]{2,1,0:T(4,128)(2,1)S(1)} all-gather(bf16[1,4,16384]{2,1,0:T(4,128)(2,1)S(1)} %bitcast.14), channel_id=1, replica_groups=mesh['groups'=2,'frame'=4,'panel'=2,'sub'=2] {'frame'}, dimensions={0}, use_global_device_ids=true | all-gather | bytes 655360 | tf_op jit(solution)/shard_map/all_gather | solution.py:12
  104.8 0.1 reshape.20
  104.9 0.2 multiply_reduce_fusion
  105.2 5.6 %fusion = f32[256,16]{0,1:T(8,128)S(1)} fusion(bf16[16,16384]{1,0:T(8,128)(2,1)S(1)} %reshape.20, bf16[256,16384]{1,0:T(8,128)(2,1)} %param.4, f32[16]{0:T(128)S(1)} %broadcast_multiply_fusion), kind=kOutput, calls=%fused_computation.3 | convolution fusion | flops 134221824 | bytes 8929344 | tf_op jit(solution)/shard_map/fp,mp->fm/dot_general | solution.py:45
  110.8 10.1 %psum.30 = f32[256,16]{0,1:T(8,128)S(1)} all-reduce(f32[256,16]{0,1:T(8,128)S(1)} %fusion), channel_id=1, replica_groups=mesh['groups'=2,'frame'=4,'panel'=2,'sub'=2] {'panel','sub'}, use_global_device_ids=true, to_apply=%region_9.10 | all-reduce | flops 4096 | bytes 32768 | tf_op jit(solution)/shard_map/psum | solution.py:48
  120.9 0.1 fusion.3
  121.0 0.1 fusion.5
  121.1 0.2 convert_reduce_fusion
  121.3 5.4 %convolution_convert_fusion = bf16[16,16384]{1,0:T(8,128)(2,1)} fusion(bf16[256,16]{0,1:T(8,128)(2,1)S(1)} %get-tuple-element.6, bf16[256,16384]{1,0:T(8,128)(2,1)} %param.4), kind=kOutput, calls=%fused_computation | convolution fusion | flops 134479872 | bytes 8921088 | tf_op jit(solution)/shard_map/fm,fp->mp/dot_general | solution.py:18
  126.7 0.0 all-reduce.7.cloned.1.call-update
  126.7 10.8 %psum.31 = f32[16]{0:T(128)S(1)} all-reduce(f32[16]{0:T(128)S(1)} %get-tuple-element.5), channel_id=1, replica_groups=mesh['groups'=2,'frame'=4,'panel'=2,'sub'=2] {'frame'}, use_global_device_ids=true, to_apply=%region_14.15 | all-reduce | flops 16 | bytes 128 | tf_op jit(solution)/shard_map/psum | solution.py:50
  137.5 0.1 dynamic-slice_add_fusion
  137.6 27.7 %all-reduce.7.cloned.1.call-done = bf16[16,16384]{1,0:T(8,128)(2,1)} async-done(((bf16[16,16384]{1,0:T(8,128)(2,1)}), bf16[16,16384]{1,0:T(8,128)(2,1)}) %all-reduce.7.cloned.1.call-update) | async-done | bytes 524304
  165.3 1.8 %add_divide_fusion = f32[4,16384]{1,0:T(4,128)} fusion(bf16[4,16384]{1,0:T(4,128)(2,1)S(1)} %fusion.1, bf16[16,16384]{1,0:T(8,128)(2,1)} %all-reduce.7.cloned.1.call-done, u32[]{:T(128)S(6)} %multiply.1, f32[4]{0:T(128)S(1)} %dynamic-slice_add_fusion), kind=kLoop, calls=%fused_computation.7 | loop fusion | flops 262144 | bytes 524308 | tf_op jit(solution)/shard_map/div | solution.py:26
  (2 shorter events, 0.0 us)
Async XLA Ops:
  6.5 34.6 %copy-start.2 = (s32[16]{0:T(128)S(1)}, s32[16]{0:T(128)}, u32[]{:S(2)}) copy-start(s32[16]{0:T(128)} %param.7) | copy-start | bytes 196
  6.5 34.6 %copy-start.1 = (f32[4096]{0:T(1024)S(1)}, f32[4096]{0:T(1024)}, u32[]{:S(2)}) copy-start(f32[4096]{0:T(1024)} %param.6) | copy-start | bytes 49156
  6.5 81.0 %all-reduce.5.cloned.1.call-start = ((), (), s32[]{:S(2)}) async-start(), calls=%async_computation | async-start | bytes 1048576
  25.3 21.9 %copy-start.3 = (u32[32]{0:T(128)S(1)}, u32[32]{0:T(128)}, u32[]{:S(2)}) copy-start(u32[32]{0:T(128)} %constant.25) | copy-start | bytes 388
  25.3 62.2 %copy-start = (f32[4,16384]{1,0:T(4,128)S(1)}, f32[4,16384]{1,0:T(4,128)}, u32[]{:S(2)}) copy-start(f32[4,16384]{1,0:T(4,128)} %param.5) | copy-start | bytes 786436
  47.2 118.2 %all-reduce.7.cloned.1.call-start = ((), (), s32[]{:S(2)}) async-start(), calls=%async_computation.1 | async-start | bytes 1048576
Sparse Core Ops, SparseCore 0:
  47.3 40.1 all-reduce.4
  126.9 38.4 all-reduce.6
where the time goes:
time: 174 us
  blocking collectives  77.1 us (44%)
  waiting for transfers between devices  54.2 us (31%)
  matrix products  22.2 us (13%)
  between operations  14.1 us (8%)
  other arithmetic  5.48 us (3%)
    unnamed x4, waiting for transfers between devices  54.2 us
    all_gather x2, blocking collectives, fetch_slices(): return lax.all_gather(owned_b, 'frame', axis=0, tiled=True)  33.5 us
    psum x2, blocking collectives, local(): counts = lax.psum(jnp.sum(weights.astype(jnp.float32), axis=0), 'frame')  23.3 us
    psum x2, blocking collectives, local(): summed = lax.psum(raw, ('panel', 'sub'))  20.2 us
    dot_general x2, matrix products, local(): jnp.einsum('fp,mp->fm', frames, gathered, preferred_element_type=jnp.floa...  11.3 us
    dot_general x2, matrix products, owner_update(): jnp.einsum('fm,fp->mp', weights, frames, preferred_element_type=jnp.float32)  10.8 us
  transfers between devices with their start and end apart: 2, of which 2 were waited for; matrix products, arithmetic and copies ran while one was open for 0% of the time, Pallas kernels for 0%

commit v1 on v0

--- a/solution.py
+++ b/solution.py
@@ -45,7 +45,12 @@
             jnp.einsum("fp,mp->fm", frames, gathered, preferred_element_type=jnp.float32)
             - 0.5 * norms[None, :]
         )
-        summed = lax.psum(raw, ("panel", "sub"))
+
+        def _turn_arrays(field_in):
+            oldest = lax.all_gather(field_in, ("panel", "sub")).sum(axis=0)
+            return oldest
+
+        summed = _turn_arrays(raw)
         weights = jax.nn.softmax(temper * summed + prior[None, :], axis=1).astype(jnp.bfloat16)
         counts = lax.psum(jnp.sum(weights.astype(jnp.float32), axis=0), "frame")
         if step + 1 < ITERS:

time: 174 us -> 165 us (0.948)
  blocking collectives: 77.1 us -> 67.4 us
    psum x2 -> x0, blocking collectives: 20.2 us -> none  [local(): summed = lax.psum(raw, ('panel', 'sub'))]
    all_gather x0 -> x2, blocking collectives: none -> 10.5 us  [_turn_arrays(): oldest = lax.all_gather(field_in, ('panel', 'sub')).sum(axis=0)]
where the time goes in v1:
time: 165 us; the launch traced here: 164 us
  blocking collectives  67.4 us (41%)
  waiting for transfers between devices  53.9 us (33%)
  matrix products  22.2 us (13%)
  between operations  14.2 us (9%)
  other arithmetic  5.55 us (3%)
    unnamed x4, waiting for transfers between devices  53.9 us
    all_gather x2, blocking collectives, fetch_slices(): return lax.all_gather(owned_b, 'frame', axis=0, tiled=True)  33.5 us
    psum x2, blocking collectives, local(): counts = lax.psum(jnp.sum(weights.astype(jnp.float32), axis=0), 'frame')  23.3 us
    dot_general x2, matrix products, local(): jnp.einsum('fp,mp->fm', frames, gathered, preferred_element_type=jnp.floa...  11.3 us
    dot_general x2, matrix products, owner_update(): jnp.einsum('fm,fp->mp', weights, frames, preferred_element_type=jnp.float32)  10.8 us
    all_gather x2, blocking collectives, _turn_arrays(): oldest = lax.all_gather(field_in, ('panel', 'sub')).sum(axis=0)  10.5 us
  transfers between devices with their start and end apart: 2, of which 2 were waited for; matrix products, arithmetic and copies ran while one was open for 0% of the time, Pallas kernels for 0%

profile of v1, /device:TPU:0, one launch (start us, length us, event | category | flops | bytes accessed | tf_op | source)
XLA Modules:
  0.0 164.1 jit_solution(12453963066606732000)
XLA Ops:
  6.5 0.0 copy-start.2
  6.5 0.0 copy-start.1
  6.5 0.0 all-reduce.5.cloned.1.call-start
  6.5 1.0 convert_bitcast_fusion
  7.6 17.4 %all-gather.2 = bf16[4,4,16384]{2,1,0:T(4,128)(2,1)S(1)} all-gather(bf16[1,4,16384]{2,1,0:T(4,128)(2,1)S(1)} %convert_bitcast_fusion), channel_id=1, replica_groups=mesh['groups'=2,'frame'=4,'panel'=2,'sub'=2] {'frame'}, dimensions={0}, use_global_device_ids=true | all-gather | bytes 655360 | tf_op jit(solution)/shard_map/all_gather | solution.py:12
  24.9 0.1 reshape.20
  25.1 0.2 multiply_reduce_fusion.1
  25.3 0.0 copy-start.3
  25.3 0.0 copy-start
  25.3 5.7 %convolution_subtract_fusion.1 = f32[256,16]{0,1:T(8,128)S(1)} fusion(bf16[256,16384]{1,0:T(8,128)(2,1)} %param.4, bf16[16,16384]{1,0:T(8,128)(2,1)S(1)} %reshape.20, f32[16]{0:T(128)S(1)} %broadcast_multiply_fusion.1), kind=kOutput, calls=%fused_computation.4 | convolution fusion | flops 134221824 | bytes 8929344 | tf_op jit(solution)/shard_map/fp,mp->fm/dot_general | solution.py:45
  31.0 5.2 %all-gather = f32[1024,16]{0,1:T(8,128)S(1)} all-gather(f32[256,16]{0,1:T(8,128)S(1)} %convolution_subtract_fusion.1), channel_id=2, replica_groups=mesh['groups'=2,'frame'=4,'panel'=2,'sub'=2] {'panel','sub'}, dimensions={0}, use_global_device_ids=true | all-gather | bytes 81920 | tf_op jit(solution)/shard_map/all_gather | solution.py:50
  36.3 0.0 copy-done.2
  36.3 0.0 copy-done.1
  36.3 0.2 select_reduce_fusion
  36.6 0.1 fusion.2
  36.7 0.1 fusion.4
  36.8 0.2 convert_reduce_fusion.1
  37.0 5.4 %convolution_convert_fusion.1 = bf16[16,16384]{1,0:T(8,128)(2,1)} fusion(bf16[256,16]{0,1:T(8,128)(2,1)S(1)} %get-tuple-element.8, bf16[256,16384]{1,0:T(8,128)(2,1)} %param.4), kind=kOutput, calls=%fused_computation.1 | convolution fusion | flops 134479872 | bytes 8921088 | tf_op jit(solution)/shard_map/fm,fp->mp/dot_general | solution.py:18
  42.4 0.0 all-reduce.5.cloned.1.call-update
  42.4 0.0 all-reduce.7.cloned.1.call-start
  42.5 0.0 copy-done.3
  42.5 0.6 dynamic-slice
  43.7 12.6 %psum.14 = f32[16]{0:T(128)S(1)} all-reduce(f32[16]{0:T(128)S(1)} %get-tuple-element.7), channel_id=1, replica_groups=mesh['groups'=2,'frame'=4,'panel'=2,'sub'=2] {'frame'}, use_global_device_ids=true, to_apply=%region_7.8 | all-reduce | flops 16 | bytes 128 | tf_op jit(solution)/shard_map/psum | solution.py:55
  56.3 0.1 dynamic-slice_add_fusion.1
  56.3 26.4 %all-reduce.5.cloned.1.call-done = bf16[16,16384]{1,0:T(8,128)(2,1)} async-done(((bf16[16,16384]{1,0:T(8,128)(2,1)}), bf16[16,16384]{1,0:T(8,128)(2,1)}) %all-reduce.5.cloned.1.call-update) | async-done | bytes 524304
  82.7 0.0 copy-done
  82.7 1.1 fusion.1
  83.8 16.2 %all-gather.3 = bf16[4,4,16384]{2,1,0:T(4,128)(2,1)S(1)} all-gather(bf16[1,4,16384]{2,1,0:T(4,128)(2,1)S(1)} %bitcast.18), channel_id=1, replica_groups=mesh['groups'=2,'frame'=4,'panel'=2,'sub'=2] {'frame'}, dimensions={0}, use_global_device_ids=true | all-gather | bytes 655360 | tf_op jit(solution)/shard_map/all_gather | solution.py:12
  99.9 0.1 reshape.22
  100.1 0.2 multiply_reduce_fusion
  100.3 5.6 %fusion = f32[256,16]{0,1:T(8,128)S(1)} fusion(bf16[16,16384]{1,0:T(8,128)(2,1)S(1)} %reshape.22, bf16[256,16384]{1,0:T(8,128)(2,1)} %param.4, f32[16]{0:T(128)S(1)} %broadcast_multiply_fusion), kind=kOutput, calls=%fused_computation.3 | convolution fusion | flops 134221824 | bytes 8929344 | tf_op jit(solution)/shard_map/fp,mp->fm/dot_general | solution.py:45
  106.0 5.2 %all-gather.1 = f32[1024,16]{0,1:T(8,128)S(1)} all-gather(f32[256,16]{0,1:T(8,128)S(1)} %fusion), channel_id=3, replica_groups=mesh['groups'=2,'frame'=4,'panel'=2,'sub'=2] {'panel','sub'}, dimensions={0}, use_global_device_ids=true | all-gather | bytes 81920 | tf_op jit(solution)/shard_map/all_gather | solution.py:50
  111.3 0.1 fusion.3
  111.4 0.1 fusion.5
  111.5 0.2 convert_reduce_fusion
  111.7 5.4 %convolution_convert_fusion = bf16[16,16384]{1,0:T(8,128)(2,1)} fusion(bf16[256,16]{0,1:T(8,128)(2,1)S(1)} %get-tuple-element.6, bf16[256,16384]{1,0:T(8,128)(2,1)} %param.4), kind=kOutput, calls=%fused_computation | convolution fusion | flops 134479872 | bytes 8921088 | tf_op jit(solution)/shard_map/fm,fp->mp/dot_general | solution.py:18
  117.1 0.0 all-reduce.7.cloned.1.call-update
  117.1 10.8 %psum.15 = f32[16]{0:T(128)S(1)} all-reduce(f32[16]{0:T(128)S(1)} %get-tuple-element.5), channel_id=1, replica_groups=mesh['groups'=2,'frame'=4,'panel'=2,'sub'=2] {'frame'}, use_global_device_ids=true, to_apply=%region_14.15 | all-reduce | flops 16 | bytes 128 | tf_op jit(solution)/shard_map/psum | solution.py:55
  127.9 0.1 dynamic-slice_add_fusion
  128.0 27.6 %all-reduce.7.cloned.1.call-done = bf16[16,16384]{1,0:T(8,128)(2,1)} async-done(((bf16[16,16384]{1,0:T(8,128)(2,1)}), bf16[16,16384]{1,0:T(8,128)(2,1)}) %all-reduce.7.cloned.1.call-update) | async-done | bytes 524304
  155.5 1.8 %add_divide_fusion = f32[4,16384]{1,0:T(4,128)} fusion(bf16[4,16384]{1,0:T(4,128)(2,1)S(1)} %fusion.1, bf16[16,16384]{1,0:T(8,128)(2,1)} %all-reduce.7.cloned.1.call-done, u32[]{:T(128)S(6)} %multiply.1, f32[4]{0:T(128)S(1)} %dynamic-slice_add_fusion), kind=kLoop, calls=%fused_computation.7 | loop fusion | flops 262144 | bytes 524308 | tf_op jit(solution)/shard_map/div | solution.py:26
  (6 shorter events, 0.2 us)
Async XLA Ops:
  6.5 29.8 %copy-start.2 = (s32[16]{0:T(128)S(1)}, s32[16]{0:T(128)}, u32[]{:S(2)}) copy-start(s32[16]{0:T(128)} %param.7) | copy-start | bytes 196
  6.5 29.8 %copy-start.1 = (f32[4096]{0:T(1024)S(1)}, f32[4096]{0:T(1024)}, u32[]{:S(2)}) copy-start(f32[4096]{0:T(1024)} %param.6) | copy-start | bytes 49156
  6.5 76.2 %all-reduce.5.cloned.1.call-start = ((), (), s32[]{:S(2)}) async-start(), calls=%async_computation | async-start | bytes 1048576
  25.3 17.2 %copy-start.3 = (u32[32]{0:T(128)S(1)}, u32[32]{0:T(128)}, u32[]{:S(2)}) copy-start(u32[32]{0:T(128)} %constant.25) | copy-start | bytes 388
  25.3 57.4 %copy-start = (f32[4,16384]{1,0:T(4,128)S(1)}, f32[4,16384]{1,0:T(4,128)}, u32[]{:S(2)}) copy-start(f32[4,16384]{1,0:T(4,128)} %param.5) | copy-start | bytes 786436
  42.4 113.1 %all-reduce.7.cloned.1.call-start = ((), (), s32[]{:S(2)}) async-start(), calls=%async_computation.1 | async-start | bytes 1048576
Sparse Core Ops, SparseCore 0:
  42.5 40.1 all-reduce.4
  117.2 38.2 all-reduce.6
